TPU v7x, 32 devices: a whole 2x2x4 slice. The times are simulated.
32 devices in a mesh: sp: 4 (over y, x), ep: 8 (over z, core).
Axes of the slice: x: 2, y: 2, z: 4, core: 2. Of those that a mesh axis runs over, the one named last changes fastest.
Arguments:
- residual: bfloat16 [4096, 4096], P(('sp', 'ep')), may hold values from -40 to 40
- queries: bfloat16 [4096, 4096], P(('sp', 'ep')), may hold values from -6 to 6
- key_rows: bfloat16 [4096, 1024], P(('sp', 'ep')), may hold values from -6 to 6
- value_rows: bfloat16 [4096, 1024], P(('sp', 'ep')), may hold values from -6 to 6
- visible: int32 [32, 5], replicated, may hold values from 0 to 1, as said below
- out_proj: bfloat16 [4096, 4096], P(('sp', 'ep')), may hold values from -0.09375 to 0.09375
- norm_gain: float32 [4096], replicated, may hold values from 0.5 to 1.5
- expert_ids: int32 [4096, 2], P(('sp', 'ep')), may hold values from 0 to 7, all different within a row; in each aligned block of 128 rows (0 to 127, 128 to 255, ...) at most 40 rows name the same one
- route_weight: float32 [4096, 2], P(('sp', 'ep')), may hold values from 0.2 to 1
- expert_gate: bfloat16 [2, 7168, 4096], P(None, 'ep'), may hold values from -0.09375 to 0.09375
- expert_up: bfloat16 [2, 7168, 4096], P(None, 'ep'), may hold values from -0.09375 to 0.09375
- expert_down: bfloat16 [2, 7168, 4096], P(None, 'ep'), may hold values from -0.0625 to 0.0625
Outputs:
- layer_out: bfloat16 [4096, 4096], P(('sp', 'ep'))
Inputs may be any that keep to these rules, and one draw needn't show every extreme that they name: The sequence is packed with documents that are runs of whole blocks of 128 tokens, the first of them 5 blocks or longer; visible[q, d] is 1 exactly when block q - d exists and lies in the document of block q, so visible[q, 0] = 1. `expert_ids`: each token names two different experts. Among the 128 tokens of one block no expert is named by more than 40 tokens.
All inputs are finite; a program needn't handle non-finite values.
Results may differ from a plain program's by a relative error of at most 0.0065.
Values may be sent and summed in bfloat16 or wider, within the bound.
A program may use at most 128 MiB of HBM per device.

v0:
```python
import math
import jax
import jax.numpy as jnp
from jax import lax
from jax.sharding import PartitionSpec as P

HEAD = 128
CAP = 40


def settle(shard_piece, distance, ep_index):
    lowered = jnp.concatenate([jnp.zeros_like(shard_piece[:1]), shard_piece[:-1]], axis=0)
    return jnp.where(distance > ep_index, lowered, shard_piece)


def local(
    residual,
    queries,
    key_rows,
    value_rows,
    visible,
    out_proj,
    norm_gain,
    expert_ids,
    route_weight,
    expert_gate,
    expert_up,
    expert_down,
):
    sp_count = lax.axis_size("sp")
    ep_count = lax.axis_size("ep")
    ep_index = lax.axis_index("ep")
    tokens = residual.shape[0]
    reach = ep_count // 2 + 1
    query_width = queries.shape[1] // sp_count
    key_width = key_rows.shape[1] // sp_count
    key_heads = key_width // HEAD
    grouping = query_width // key_width
    query_send = queries.reshape(1, tokens, sp_count, query_width)
    key_send = key_rows.reshape(1, tokens, sp_count, key_width)
    value_send = value_rows.reshape(1, tokens, sp_count, key_width)
    query_heads, key_local, value_local = (
        lax.all_to_all(query_send, "sp", split_axis=2, concat_axis=0, tiled=True),
        lax.all_to_all(key_send, "sp", split_axis=2, concat_axis=0, tiled=True),
        lax.all_to_all(value_send, "sp", split_axis=2, concat_axis=0, tiled=True),
    )
    key_value = jnp.concatenate(
        [
            key_local.reshape(sp_count, tokens, key_width),
            value_local.reshape(sp_count, tokens, key_width),
        ],
        axis=2,
    )
    pieces = [key_value]
    gathered = lax.all_gather(key_value[None], "ep", axis=0, tiled=True)
    for distance in range(1, reach):
        source = (ep_index - distance) % ep_count
        pieces.append(
            settle(
                lax.dynamic_index_in_dim(gathered, source, 0, keepdims=False), distance, ep_index
            )
        )
    window = jnp.stack(pieces, axis=0)
    key_window = window[..., :key_width].reshape(reach, sp_count, tokens, key_heads, HEAD)
    value_window = window[..., key_width:].reshape(reach, sp_count, tokens, key_heads, HEAD)
    query_local = query_heads.reshape(sp_count, tokens, key_heads, grouping, HEAD)
    scores = jnp.einsum(
        "stgrh,dsugh->sgrtdu", query_local, key_window, preferred_element_type=jnp.float32
    ) * (1.0 / math.sqrt(HEAD))
    seen = lax.dynamic_index_in_dim(
        visible.reshape(sp_count, ep_count, reach), ep_index, 1, keepdims=False
    )
    position = jnp.arange(tokens)
    distances = jnp.arange(reach)
    allowed = (seen[:, None, :, None] > 0) & (
        (distances[None, None, :, None] > 0)
        | (position[None, None, None, :] <= position[None, :, None, None])
    )
    allowed = allowed[:, None, None]
    scores = jnp.where(allowed, scores, -1e30)
    peak = jnp.max(scores, axis=(4, 5), keepdims=True)
    weights_f = jnp.where(allowed, jnp.exp(scores - peak), 0.0)
    totals = jnp.sum(weights_f, axis=(4, 5))
    weights_b = weights_f.astype(jnp.bfloat16)
    summed = jnp.einsum(
        "sgrtdu,dsugh->stgrh", weights_b, value_window, preferred_element_type=jnp.float32
    )
    attended = (summed / jnp.transpose(totals, (0, 3, 1, 2))[..., None]).astype(jnp.bfloat16)
    attended = attended.reshape(sp_count * tokens, query_width)
    proj_full = lax.all_gather(out_proj, "ep", axis=0, tiled=True)
    projected = lax.psum_scatter(
        jnp.dot(attended, proj_full, preferred_element_type=jnp.float32).astype(jnp.bfloat16),
        "sp",
        scatter_dimension=0,
        tiled=True,
    ).astype(jnp.float32)
    hidden_sum = residual.astype(jnp.float32) + projected
    mean_square = jnp.mean(hidden_sum * hidden_sum, axis=-1, keepdims=True)
    normed = (hidden_sum * lax.rsqrt(mean_square + 1e-05) * norm_gain).astype(jnp.bfloat16)
    window_experts = expert_gate.shape[0]
    capacity = CAP
    choose = expert_ids[None] == jnp.arange(window_experts, dtype=jnp.int32)[:, None, None]
    member = jnp.any(choose, axis=2)
    token_weight = jnp.sum(jnp.where(choose, route_weight[None], 0.0), axis=2)
    ranked = jnp.cumsum(member.astype(jnp.int32), axis=1) - member.astype(jnp.int32)
    slot_hit = (
        ranked[:, None, :] == jnp.arange(capacity, dtype=jnp.int32)[None, :, None]
    ) & member[:, None, :]
    dispatch = slot_hit.astype(jnp.bfloat16)
    outgoing = jnp.einsum(
        "wct,td->wcd", dispatch, normed, preferred_element_type=jnp.float32
    ).astype(jnp.bfloat16)
    combine = jnp.where(slot_hit, token_weight[:, None, :], 0.0)
    shard_piece = lax.all_gather(outgoing, "ep", axis=1, tiled=True)
    gate_act = jnp.einsum(
        "wnd,wfd->wnf", shard_piece, expert_gate, preferred_element_type=jnp.float32
    )
    up_act = jnp.einsum("wnd,wfd->wnf", shard_piece, expert_up, preferred_element_type=jnp.float32)
    activated = (jax.nn.silu(gate_act) * up_act).astype(jnp.bfloat16)
    partial_value = jnp.einsum(
        "wnf,wfd->wnd", activated, expert_down, preferred_element_type=jnp.float32
    )
    returned = lax.psum_scatter(
        partial_value.astype(jnp.bfloat16), "ep", scatter_dimension=1, tiled=True
    ).astype(jnp.float32)
    expert_mix = jnp.einsum("wct,wcd->td", combine, returned, precision=lax.Precision.HIGHEST)
    return (hidden_sum + expert_mix).astype(jnp.bfloat16)


def solution(mesh):
    return jax.shard_map(
        local,
        mesh=mesh,
        in_specs=(
            P(("sp", "ep"), None),
            P(("sp", "ep"), None),
            P(("sp", "ep"), None),
            P(("sp", "ep"), None),
            P(),
            P(("sp", "ep"), None),
            P(),
            P(("sp", "ep"), None),
            P(("sp", "ep"), None),
            P(None, "ep", None),
            P(None, "ep", None),
            P(None, "ep", None),
        ),
        out_specs=P(("sp", "ep"), None),
        check_vma=False,
    )
```

profile of v0, /device:TPU:0, one launch (start us, length us, event | category | flops | bytes accessed | tf_op | source)
XLA Modules:
  0.0 411.7 jit_solution(12363634068117116235)
XLA Ops:
  6.5 1.8 copy.45
  8.3 5.3 %all-to-all-start = ((bf16[1,128,4,256]{1,3,0,2:T(8,128)(2,1)}), bf16[1,128,4,256]{1,3,0,2:T(8,128)(2,1)S(1)}, u32[]{:S(2)}, u32[]{:S(2)}) async-start(bf16[1,128,4,256]{1,3,0,2:T(8,128)(2,1)} %bitcast), calls=%async_computation | async-start | bytes 524288 | tf_op jit(solution)/shard_map/all_to_all | solution.py:44
  13.7 1.1 copy.46
  14.8 4.2 %all-to-all-done = bf16[1,128,4,256]{1,3,0,2:T(8,128)(2,1)S(1)} async-done(((bf16[1,128,4,256]{1,3,0,2:T(8,128)(2,1)}), bf16[1,128,4,256]{1,3,0,2:T(8,128)(2,1)S(1)}, u32[]{:S(2)}, u32[]{:S(2)}) %all-to-all-start) | async-done | bytes 262176 | tf_op jit(solution)/shard_map/all_to_all | solution.py:44
  19.0 8.1 %all_to_all.45 = bf16[1,128,4,256]{1,3,0,2:T(8,128)(2,1)S(1)} all-to-all(bf16[1,128,4,256]{1,3,0,2:T(8,128)(2,1)S(1)} %bitcast.130), channel_id=1, replica_groups=mesh['sp'=4,'ep'=8] {'sp'}, dimensions={2} | all-to-all | bytes 524288 | tf_op jit(solution)/shard_map/all_to_all | solution.py:45
  27.2 1.0 copy.47
  28.3 0.7 all-gather.5.cloned.1.call-update
  29.0 1.3 copy.50
  30.3 3.5 all-to-all-start.2
  33.8 0.0 reduce-scatter.5.cloned.1.call-start
  34.0 0.1 reshape.106
  34.1 0.1 constant_dynamic-slice_fusion
  34.1 0.1 copy.70
  34.3 0.1 broadcast_or_fusion
  34.4 1.0 broadcast_and_fusion
  35.4 0.8 bitcast_dynamic-update-slice_fusion.4
  36.2 38.7 %all-gather.9.cloned.1.call-done = bf16[32,128,512]{2,1,0:T(8,128)(2,1)} async-done(((bf16[4,128,512]{2,1,0:T(8,128)(2,1)}), bf16[32,128,512]{2,1,0:T(8,128)(2,1)}) %all-gather.9.cloned.1.call-update) | async-done | bytes 4194320 | tf_op jit(solution)/shard_map/all_gather | solution.py:55
  75.0 6.4 %copy.48 = bf16[32,128,512]{1,2,0:T(8,128)(2,1)} copy(bf16[32,128,512]{2,1,0:T(8,128)(2,1)} %all-gather.9.cloned.1.call-done) | data formatting | bytes 8388608 | tf_op jit(solution)/shard_map/all_gather | solution.py:55
  81.4 1.7 dynamic-slice_bitcast_fusion
  83.2 0.9 copy-done.2
  84.0 1.3 bitcast_dynamic-update-slice_fusion.3
  85.4 1.3 bitcast_dynamic-update-slice_fusion.2
  86.6 1.2 bitcast_dynamic-update-slice_fusion.1
  87.8 1.2 bitcast_dynamic-update-slice_fusion
  89.1 1.3 fusion.30
  90.3 2.7 fusion
  93.0 6.6 %fusion.1 = (f32[4,2,4,128]{3,2,1,0:T(4,128)S(1)}, bf16[4,2,4,128,5,128]{3,5,2,4,1,0:T(8,128)(2,1)}) fusion(f32[4,2,5,128,128,4]{4,3,5,2,1,0:T(8,128)S(1)} %get-tuple-element.14, f32[4,2,4,128]{3,2,1,0:T(4,128)S(1)} %get-tuple-element.13, pred[4,128,5,128]{1,3,2,0:T(8,128)(4,1)} %broadcast_and_fusion), kind=kLoop, calls=%fused_computation.3 | loop fusion | flops 15724544 | bytes 16089088 | tf_op jit(solution)/shard_map/reduce_sum | solution.py:83
  99.6 3.5 fusion.7
  103.2 0.7 copy.55
  103.9 0.8 reshape.110
  104.7 52.8 %all-gather.5.cloned.1.call-done = bf16[1024,4096]{1,0:T(8,128)(2,1)} async-done(((bf16[128,4096]{1,0:T(8,128)(2,1)}), bf16[1024,4096]{1,0:T(8,128)(2,1)}) %all-gather.5.cloned.1.call-update) | async-done | bytes 8388624 | tf_op jit(solution)/shard_map/all_gather | solution.py:90
  157.4 9.4 %convolution_convert_fusion.1 = bf16[512,4096]{1,0:T(8,128)(2,1)} fusion(bf16[512,1024]{1,0:T(8,128)(2,1)S(1)} %reshape.110, bf16[1024,4096]{1,0:T(8,128)(2,1)} %all-gather.5.cloned.1.call-done), kind=kOutput, calls=%fused_computation.6 | convolution fusion | flops 4297064448 | bytes 13631488 | tf_op jit(solution)/shard_map/dot_general | solution.py:92
  166.9 0.2 all-gather.7.cloned.1.call-start
  167.1 0.4 copy-done.7
  167.5 0.3 reduce_window_sum.11
  167.8 50.3 %reduce-scatter.5.cloned.1.call-done = bf16[128,4096]{1,0:T(8,128)(2,1)} async-done(((bf16[512,4096]{1,0:T(8,128)(2,1)}), bf16[128,4096]{1,0:T(8,128)(2,1)}) %reduce-scatter.5.cloned.1.call-update) | async-done | bytes 1048592 | tf_op jit(solution)/shard_map/reduce_scatter | solution.py:91
  218.1 1.6 multiply_reduce_fusion
  219.8 2.7 convolution_convert_fusion.2
  222.5 0.0 reduce-scatter.7.cloned.1.call-start
  222.5 56.1 %all-gather.7.cloned.1.call-done = bf16[2,320,4096]{2,1,0:T(8,128)(2,1)} async-done(((bf16[2,40,4096]{2,1,0:T(8,128)(2,1)}), bf16[2,320,4096]{2,1,0:T(8,128)(2,1)}) %all-gather.7.cloned.1.call-update) | async-done | bytes 5242896 | tf_op jit(solution)/shard_map/all_gather | solution.py:114
  278.6 16.7 %fusion.31 = f32[2,320,896]{2,1,0:T(8,128)} fusion(bf16[2,320,4096]{2,1,0:T(8,128)(2,1)} %all-gather.7.cloned.1.call-done, bf16[2,896,4096]{2,1,0:T(8,128)(2,1)} %param.21), kind=kOutput, calls=%fused_computation.62 | convolution fusion | flops 4697620480 | bytes 22216704 | tf_op jit(solution)/shard_map/wnd,wfd->wnf/dot_general | solution.py:115
  295.3 25.4 %convolution_convert_fusion = bf16[2,320,4096]{2,1,0:T(8,128)(2,1)} fusion(bf16[2,896,4096]{2,1,0:T(8,128)(2,1)} %param.23, f32[2,320,896]{2,1,0:T(8,128)} %fusion.31, bf16[2,320,4096]{2,1,0:T(8,128)(2,1)} %all-gather.7.cloned.1.call-done, bf16[2,896,4096]{2,1,0:T(8,128)(2,1)} %param.22), kind=kOutput, calls=%fused_computation.5 | convolution fusion | flops 9401303040 | bytes 42139648 | tf_op jit(solution)/shard_map/wnf,wfd->wnd/dot_general | solution.py:120
  320.7 10.3 %copy.68 = bf16[2,320,4096]{2,0,1:T(2,128)(2,1)} copy(bf16[2,320,4096]{2,1,0:T(8,128)(2,1)} %convolution_convert_fusion) | data formatting | bytes 10485760
  331.1 10.7 %copy.71 = bf16[40,8,2,4096]{3,1,2,0:T(8,128)(2,1)} copy(bf16[40,8,2,4096]{3,2,1,0:T(2,128)(2,1)} %bitcast.116) | data formatting | bytes 10485760
  341.8 0.7 copy-done.8
  342.5 58.1 %reduce-scatter.7.cloned.1.call-done = bf16[40,8192]{1,0:T(8,128)(2,1)} async-done(((bf16[320,8192]{1,0:T(8,128)(2,1)}), bf16[40,8192]{1,0:T(8,128)(2,1)}) %reduce-scatter.7.cloned.1.call-update) | async-done | bytes 655376
  400.6 2.3 reshape.119
  402.9 2.2 fusion.6
  (31 shorter events, 0.3 us)
Async XLA Ops:
  8.3 20.7 %copy-start.4 = (bf16[128,4096]{1,0:T(8,128)(2,1)S(1)}, bf16[128,4096]{1,0:T(8,128)(2,1)}, u32[]{:S(2)}) copy-start(bf16[128,4096]{1,0:T(8,128)(2,1)} %param.13) | copy-start | bytes 3145732
  8.3 10.7 %all-to-all-start = ((bf16[1,128,4,256]{1,3,0,2:T(8,128)(2,1)}), bf16[1,128,4,256]{1,3,0,2:T(8,128)(2,1)S(1)}, u32[]{:S(2)}, u32[]{:S(2)}) async-start(bf16[1,128,4,256]{1,3,0,2:T(8,128)(2,1)} %bitcast), calls=%async_computation | async-start | bytes 524288 | tf_op jit(solution)/shard_map/all_to_all | solution.py:44
  13.7 61.3 %all-gather.9.cloned.1.call-start = ((), (), s32[]{:S(2)}) async-start(), calls=%async_computation.8 | async-start | bytes 4718592 | tf_op jit(solution)/shard_map/all_gather | solution.py:55
  28.2 5.8 %copy-start.6 = (s32[32,5]{0,1:T(8,128)S(1)}, s32[32,5]{0,1:T(8,128)}, u32[]{:S(2)}) copy-start(s32[32,5]{0,1:T(8,128)} %param.16) | copy-start | bytes 1924
  28.2 129.2 %all-gather.5.cloned.1.call-start = ((), (), s32[]{:S(2)}) async-start(), calls=%async_computation.5 | async-start | bytes 9437184 | tf_op jit(solution)/shard_map/all_gather | solution.py:90
  30.3 60.0 %all-to-all-start.2 = ((bf16[1,128,4,1024]{1,3,0,2:T(8,128)(2,1)}), bf16[1,128,4,1024]{1,3,0,2:T(8,128)(2,1)S(1)}, u32[]{:S(2)}, u32[]{:S(2)}) async-start(bf16[1,128,4,1024]{1,3,0,2:T(8,128)(2,1)} %bitcast.27), calls=%async_computation.2 | async-start | bytes 2097152 | tf_op jit(solution)/shard_map/all_to_all | solution.py:43
  33.8 184.3 %reduce-scatter.5.cloned.1.call-start = ((), (), s32[]{:S(2)}) async-start(), calls=%async_computation.6 | async-start | bytes 5242880 | tf_op jit(solution)/shard_map/reduce_scatter | solution.py:91
  81.4 2.6 copy-start.2
  93.0 6.6 %copy-start.3 = (bf16[5,4,128,256]{2,3,1,0:T(8,128)(2,1)S(1)}, bf16[5,4,128,256]{2,3,1,0:T(8,128)(2,1)}, u32[]{:S(2)}) copy-start(bf16[5,4,128,256]{2,3,1,0:T(8,128)(2,1)} %get-tuple-element.11) | copy-start | bytes 3932164
  166.8 0.7 copy-start.7
  166.8 51.3 %copy-start = (bf16[128,4096]{1,0:T(8,128)(2,1)S(1)}, bf16[128,4096]{1,0:T(8,128)(2,1)}, u32[]{:S(2)}) copy-start(bf16[128,4096]{1,0:T(8,128)(2,1)} %param.12) | copy-start | bytes 3145732
  166.8 52.9 %copy-start.5 = (f32[4096]{0:T(1024)S(1)}, f32[4096]{0:T(1024)}, u32[]{:S(2)}) copy-start(f32[4096]{0:T(1024)} %param.18) | copy-start | bytes 49156
  166.9 111.7 %all-gather.7.cloned.1.call-start = ((), (), s32[]{:S(2)}) async-start(), calls=%async_computation.7 | async-start | bytes 5898240 | tf_op jit(solution)/shard_map/all_gather | solution.py:114
  222.5 178.1 %reduce-scatter.7.cloned.1.call-start = ((), (), s32[]{:S(2)}) async-start(), calls=%async_computation.9 | async-start | bytes 5898240
  341.8 0.7 copy-start.8
  341.8 61.1 %copy-start.1 = (bf16[128,4096]{1,0:T(8,128)(2,1)S(1)}, bf16[128,4096]{1,0:T(8,128)(2,1)}, u32[]{:S(2)}) copy-start(bf16[128,4096]{1,0:T(8,128)(2,1)} %reduce-scatter.5.cloned.1.call-done) | copy-start | bytes 3145732
Sparse Core Ops, SparseCore 0:
  28.3 46.5 all-gather.8
  76.6 80.8 all-gather.4
  167.0 51.0 reduce-scatter.4
  222.6 55.9 all-gather.6
  341.9 58.5 reduce-scatter.6
where the time goes:
time: 413 us; the launch traced here: 412 us
  waiting for transfers between devices  261 us (63%)
  matrix products  62.7 us (15%)
  local copies, waits for them, and re-layouts  41.8 us (10%)
  other arithmetic  15.6 us (4%)
  between operations  13.4 us (3%)
  starting transfers between devices  9.19 us (2%)
  blocking collectives  8.1 us (2%)
    unnamed x6, waiting for transfers between devices  58.8 us
    all_gather x1, waiting for transfers between devices, local(): shard_piece = lax.all_gather(outgoing, 'ep', axis=1, tiled=True)  56.1 us
    all_gather x1, waiting for transfers between devices, local(): proj_full = lax.all_gather(out_proj, 'ep', axis=0, tiled=True)  52.8 us
    reduce_scatter x1, waiting for transfers between devices, local(): lax.psum_scatter(jnp.dot(attended, proj_full, preferred_element_type=jnp....  50.3 us
    all_gather x1, waiting for transfers between devices, local(): gathered = lax.all_gather(key_value[None], 'ep', axis=0, tiled=True)  38.7 us
    unnamed x25, local copies, waits for them, and re-layouts  29.7 us
    dot_general x1, matrix products, local(): jnp.einsum('wnf,wfd->wnd', activated, expert_down, preferred_element_type...  25.4 us
    dot_general x1, matrix products, local(): jnp.einsum('wnd,wfd->wnf', shard_piece, expert_gate, preferred_element_ty...  16.7 us
  transfers between devices with their start and end apart: 7, of which 6 were waited for; matrix products, arithmetic and copies ran while one was open for 8% of the time, Pallas kernels for 0%

commit v1 on v0

--- a/solution.py
+++ b/solution.py
@@ -87,7 +87,24 @@
     )
     attended = (summed / jnp.transpose(totals, (0, 3, 1, 2))[..., None]).astype(jnp.bfloat16)
     attended = attended.reshape(sp_count * tokens, query_width)
-    proj_full = lax.all_gather(out_proj, "ep", axis=0, tiled=True)
+
+    def point_zone(message, shard_axis):
+        p_count = lax.axis_size(shard_axis)
+        rack = [message]
+        for dev in [*range(p_count - 1)]:
+            rack.append(
+                lax.ppermute(
+                    rack[-1],
+                    axis_name=shard_axis,
+                    perm=[(w, (w + 1) % p_count) for w in range(p_count)],
+                )
+            )
+        far_arr = jnp.roll(
+            jnp.concatenate(rack[::-1], 0), (lax.axis_index(shard_axis) + 1) * message.shape[0], 0
+        )
+        return far_arr
+
+    proj_full = point_zone(out_proj, "ep")
     projected = lax.psum_scatter(
         jnp.dot(attended, proj_full, preferred_element_type=jnp.float32).astype(jnp.bfloat16),
         "sp",

time: 413 us -> 464 us (1.12)
  local copies, waits for them, and re-layouts: 41.8 us -> 69.7 us
  waiting for transfers between devices: 261 us -> 279 us
  blocking collectives: 8.1 us -> 0 us
  other arithmetic: 15.6 us -> 21.5 us
    ppermute x0 -> x7, waiting for transfers between devices: none -> 85.7 us  [point_zone(): lax.ppermute(rack[-1], axis_name=shard_axis, perm=[(w, (w + 1) % p_count)...]
    all_gather x1 -> x0, waiting for transfers between devices: 52.8 us -> none  [local(): proj_full = lax.all_gather(out_proj, 'ep', axis=0, tiled=True)]
    unnamed x25 -> x50, local copies, waits for them, and re-layouts: 29.7 us -> 53.3 us
    all_gather x1, waiting for transfers between devices: 38.7 us -> 21.1 us  [local(): gathered = lax.all_gather(key_value[None], 'ep', axis=0, tiled=True)]
    all_to_all x1 -> x0, blocking collectives: 8.1 us -> none  [local(): lax.all_to_all(value_send, 'sp', split_axis=2, concat_axis=0, tiled=True)]
    all_to_all x0 -> x1, waiting for transfers between devices: none -> 7.06 us  [local(): lax.all_to_all(value_send, 'sp', split_axis=2, concat_axis=0, tiled=True)]
    unnamed x6 -> x5, waiting for transfers between devices: 58.8 us -> 58.1 us
  transfers between devices with their start and end apart: 7 -> 14, of which waited for: 6 -> 11; matrix products, arithmetic and copies ran while one was open for 8% -> 12% of each run, Pallas kernels for 0% -> 0%
where the time goes in v1:
time: 464 us; the launch traced here: 460 us
  waiting for transfers between devices  279 us (60%)
  local copies, waits for them, and re-layouts  69.7 us (15%)
  matrix products  62.9 us (14%)
  other arithmetic  21.5 us (5%)
  between operations  13.6 us (3%)
  starting transfers between devices  13.5 us (3%)
    ppermute x7, waiting for transfers between devices, point_zone(): lax.ppermute(rack[-1], axis_name=shard_axis, perm=[(w, (w + 1) % p_count)...  85.7 us
    unnamed x5, waiting for transfers between devices  58.1 us
    all_gather x1, waiting for transfers between devices, local(): shard_piece = lax.all_gather(outgoing, 'ep', axis=1, tiled=True)  56.1 us
    unnamed x50, local copies, waits for them, and re-layouts  53.3 us
    reduce_scatter x1, waiting for transfers between devices, local(): lax.psum_scatter(jnp.dot(attended, proj_full, preferred_element_type=jnp....  50.6 us
    dot_general x1, matrix products, local(): jnp.einsum('wnf,wfd->wnd', activated, expert_down, preferred_element_type...  25.6 us
    all_gather x1, waiting for transfers between devices, local(): gathered = lax.all_gather(key_value[None], 'ep', axis=0, tiled=True)  21.1 us
    dot_general x1, matrix products, local(): jnp.einsum('wnd,wfd->wnf', shard_piece, expert_gate, preferred_element_ty...  16.7 us
  transfers between devices with their start and end apart: 14, of which 11 were waited for; matrix products, arithmetic and copies ran while one was open for 12% of the time, Pallas kernels for 0%

profile of v1, /device:TPU:0, one launch (start us, length us, event | category | flops | bytes accessed | tf_op | source)
XLA Modules:
  0.0 459.9 jit_solution(6874643450508324852)
XLA Ops:
  7.0 16.7 %collective-permute-done = bf16[128,4096]{1,0:T(8,128)(2,1)S(1)} collective-permute-done((bf16[128,4096]{1,0:T(8,128)(2,1)}, bf16[128,4096]{1,0:T(8,128)(2,1)S(1)}, u32[]{:S(2)}, u32[]{:S(2)}) %collective-permute-start) | collective-permute-done | bytes 1048608 | tf_op jit(solution)/shard_map/ppermute | solution.py:96
  23.7 16.0 %collective-permute-done.1 = bf16[128,4096]{1,0:T(8,128)(2,1)S(1)} collective-permute-done((bf16[128,4096]{1,0:T(8,128)(2,1)S(1)}, bf16[128,4096]{1,0:T(8,128)(2,1)S(1)}, u32[]{:S(2)}, u32[]{:S(2)}) %collective-permute-start.1) | collective-permute-done | bytes 1048608 | tf_op jit(solution)/shard_map/ppermute | solution.py:96
  39.8 16.0 %collective-permute-done.2 = bf16[128,4096]{1,0:T(8,128)(2,1)S(1)} collective-permute-done((bf16[128,4096]{1,0:T(8,128)(2,1)S(1)}, bf16[128,4096]{1,0:T(8,128)(2,1)S(1)}, u32[]{:S(2)}, u32[]{:S(2)}) %collective-permute-start.2) | collective-permute-done | bytes 1048608 | tf_op jit(solution)/shard_map/ppermute | solution.py:96
  56.8 16.0 %collective-permute-done.3 = bf16[128,4096]{1,0:T(8,128)(2,1)S(1)} collective-permute-done((bf16[128,4096]{1,0:T(8,128)(2,1)S(1)}, bf16[128,4096]{1,0:T(8,128)(2,1)S(1)}, u32[]{:S(2)}, u32[]{:S(2)}) %collective-permute-start.3) | collective-permute-done | bytes 1048608 | tf_op jit(solution)/shard_map/ppermute | solution.py:96
  73.8 16.0 %collective-permute-done.4 = bf16[128,4096]{1,0:T(8,128)(2,1)S(1)} collective-permute-done((bf16[128,4096]{1,0:T(8,128)(2,1)S(1)}, bf16[128,4096]{1,0:T(8,128)(2,1)S(1)}, u32[]{:S(2)}, u32[]{:S(2)}) %collective-permute-start.4) | collective-permute-done | bytes 1048608 | tf_op jit(solution)/shard_map/ppermute | solution.py:96
  89.9 2.0 copy.45
  91.8 4.2 all-to-all-start
  96.0 1.8 copy.46
  98.8 2.3 copy.50
  101.1 4.9 %collective-permute-done.5 = bf16[128,4096]{1,0:T(8,128)(2,1)} collective-permute-done((bf16[128,4096]{1,0:T(8,128)(2,1)S(1)}, bf16[128,4096]{1,0:T(8,128)(2,1)}, u32[]{:S(2)}, u32[]{:S(2)}) %collective-permute-start.5) | collective-permute-done | bytes 1048608 | tf_op jit(solution)/shard_map/ppermute | solution.py:96
  106.2 4.2 all-to-all-start.1
  111.4 7.1 %all-to-all-done.1 = bf16[1,128,4,256]{1,3,0,2:T(8,128)(2,1)} async-done(((bf16[1,128,4,256]{1,3,0,2:T(8,128)(2,1)}), bf16[1,128,4,256]{1,3,0,2:T(8,128)(2,1)}, u32[]{:S(2)}, u32[]{:S(2)}) %all-to-all-start.1) | async-done | bytes 262176 | tf_op jit(solution)/shard_map/all_to_all | solution.py:45
  118.4 3.5 all-to-all-start.2
  122.0 1.9 pad_maximum_fusion
  123.9 2.1 copy.47
  126.4 2.1 bitcast_dynamic-update-slice_fusion.4
  128.4 2.3 constant_dynamic-update-slice_fusion.15
  130.7 2.4 constant_dynamic-update-slice_fusion.14
  134.1 1.1 constant_dynamic-update-slice_fusion.12
  136.2 1.1 constant_dynamic-update-slice_fusion.10
  138.4 1.1 constant_dynamic-update-slice_fusion.8
  139.5 2.4 constant_dynamic-update-slice_fusion.7
  141.9 2.3 constant_dynamic-update-slice_fusion.6
  145.2 1.1 constant_dynamic-update-slice_fusion.4
  146.3 1.1 constant_dynamic-update-slice_fusion.3
  150.5 21.1 %all-gather.6.cloned.1.call-done = bf16[32,128,512]{2,1,0:T(8,128)(2,1)} async-done(((bf16[4,128,512]{2,1,0:T(8,128)(2,1)}), bf16[32,128,512]{2,1,0:T(8,128)(2,1)}) %all-gather.6.cloned.1.call-update) | async-done | bytes 4194320 | tf_op jit(solution)/shard_map/all_gather | solution.py:55
  171.6 6.5 %copy.48 = bf16[32,128,512]{1,2,0:T(8,128)(2,1)} copy(bf16[32,128,512]{2,1,0:T(8,128)(2,1)} %all-gather.6.cloned.1.call-done) | data formatting | bytes 8388608 | tf_op jit(solution)/shard_map/all_gather | solution.py:55
  178.1 1.5 dynamic-slice_bitcast_fusion
  179.6 2.0 bitcast_dynamic-update-slice_fusion.3
  181.5 2.0 bitcast_dynamic-update-slice_fusion.2
  183.5 2.0 bitcast_dynamic-update-slice_fusion.1
  185.5 2.0 bitcast_dynamic-update-slice_fusion
  187.5 3.1 fusion.36
  190.6 2.6 fusion
  193.2 6.5 %fusion.3 = (f32[4,2,4,128]{3,2,1,0:T(4,128)S(1)}, bf16[4,2,4,128,5,128]{3,5,2,4,1,0:T(8,128)(2,1)}) fusion(f32[4,2,5,128,128,4]{4,3,5,2,1,0:T(8,128)S(1)} %get-tuple-element.14, f32[4,2,4,128]{3,2,1,0:T(4,128)S(1)} %get-tuple-element.13, pred[4,128,5,128]{1,3,2,0:T(8,128)(4,1)} %broadcast_and_fusion), kind=kLoop, calls=%fused_computation.5 | loop fusion | flops 15724544 | bytes 16089088 | tf_op jit(solution)/shard_map/reduce_sum | solution.py:83
  199.8 3.5 fusion.12
  204.8 9.5 %fusion.5 = bf16[512,4096]{1,0:T(8,128)(2,1)} fusion(bf16[512,1024]{1,0:T(8,128)(2,1)S(1)} %reshape.110, bf16[2048,4096]{1,0:T(8,128)(2,1)} %constant_dynamic-update-slice_fusion, s32[]{:T(128)S(6)} %select_n.109), kind=kOutput, calls=%fused_computation.8 | convolution fusion | flops 4297064448 | bytes 13631492 | tf_op jit(solution)/shard_map/dot_general | solution.py:109
  215.2 50.6 %reduce-scatter.5.cloned.1.call-done = bf16[128,4096]{1,0:T(8,128)(2,1)} async-done(((bf16[512,4096]{1,0:T(8,128)(2,1)}), bf16[128,4096]{1,0:T(8,128)(2,1)}) %reduce-scatter.5.cloned.1.call-update) | async-done | bytes 1048592 | tf_op jit(solution)/shard_map/reduce_scatter | solution.py:108
  265.8 1.6 multiply_reduce_fusion
  267.5 2.7 convolution_convert_fusion.1
  270.3 56.1 %all-gather.4.cloned.1.call-done = bf16[2,320,4096]{2,1,0:T(8,128)(2,1)} async-done(((bf16[2,40,4096]{2,1,0:T(8,128)(2,1)}), bf16[2,320,4096]{2,1,0:T(8,128)(2,1)}) %all-gather.4.cloned.1.call-update) | async-done | bytes 5242896 | tf_op jit(solution)/shard_map/all_gather | solution.py:131
  326.4 16.7 %fusion.37 = f32[2,320,896]{2,1,0:T(8,128)} fusion(bf16[2,320,4096]{2,1,0:T(8,128)(2,1)} %all-gather.4.cloned.1.call-done, bf16[2,896,4096]{2,1,0:T(8,128)(2,1)} %param.21), kind=kOutput, calls=%fused_computation.81 | convolution fusion | flops 4697620480 | bytes 22216704 | tf_op jit(solution)/shard_map/wnd,wfd->wnf/dot_general | solution.py:132
  343.1 25.6 %convolution_convert_fusion = bf16[2,320,4096]{2,1,0:T(8,128)(2,1)} fusion(bf16[2,896,4096]{2,1,0:T(8,128)(2,1)} %param.23, f32[2,320,896]{2,1,0:T(8,128)} %fusion.37, bf16[2,320,4096]{2,1,0:T(8,128)(2,1)} %all-gather.4.cloned.1.call-done, bf16[2,896,4096]{2,1,0:T(8,128)(2,1)} %param.22), kind=kOutput, calls=%fused_computation.7 | convolution fusion | flops 9401303040 | bytes 42139648 | tf_op jit(solution)/shard_map/wnf,wfd->wnd/dot_general | solution.py:137
  368.7 10.4 %copy.68 = bf16[2,320,4096]{2,0,1:T(2,128)(2,1)} copy(bf16[2,320,4096]{2,1,0:T(8,128)(2,1)} %convolution_convert_fusion) | data formatting | bytes 10485760
  379.0 10.7 %copy.71 = bf16[40,8,2,4096]{3,1,2,0:T(8,128)(2,1)} copy(bf16[40,8,2,4096]{3,2,1,0:T(2,128)(2,1)} %bitcast.115) | data formatting | bytes 10485760
  390.5 58.1 %reduce-scatter.7.cloned.1.call-done = bf16[40,8192]{1,0:T(8,128)(2,1)} async-done(((bf16[320,8192]{1,0:T(8,128)(2,1)}), bf16[40,8192]{1,0:T(8,128)(2,1)}) %reduce-scatter.7.cloned.1.call-update) | async-done | bytes 655376
  448.6 2.3 reshape.119
  450.9 2.2 fusion.11
  (69 shorter events, 15.5 us)
Async XLA Ops:
  6.5 17.2 %collective-permute-start = (bf16[128,4096]{1,0:T(8,128)(2,1)}, bf16[128,4096]{1,0:T(8,128)(2,1)S(1)}, u32[]{:S(2)}, u32[]{:S(2)}) collective-permute-start(bf16[128,4096]{1,0:T(8,128)(2,1)} %param.17), channel_id=1, source_target_pairs={{0,1},{1,2},{2,3},{3,4},{4,5},{5,6},{6,7},{7,0},{8,9},{9,10},{10,1... | collective-permute-start | bytes 3145736 | tf_op jit(solution)/shard_map/ppermute | solution.py:96
  23.7 16.0 %collective-permute-start.1 = (bf16[128,4096]{1,0:T(8,128)(2,1)S(1)}, bf16[128,4096]{1,0:T(8,128)(2,1)S(1)}, u32[]{:S(2)}, u32[]{:S(2)}) collective-permute-start(bf16[128,4096]{1,0:T(8,128)(2,1)S(1)} %collective-permute-done), channel_id=1, source_target_pairs={{0,1},{1,2},{2,3},{3,4},{4,5},{5,6},{6,7},{7,0},{8,9},{9,10},{10,1... | collective-permute-start | bytes 3145736 | tf_op jit(solution)/shard_map/ppermute | solution.py:96
  39.8 16.0 %collective-permute-start.2 = (bf16[128,4096]{1,0:T(8,128)(2,1)S(1)}, bf16[128,4096]{1,0:T(8,128)(2,1)S(1)}, u32[]{:S(2)}, u32[]{:S(2)}) collective-permute-start(bf16[128,4096]{1,0:T(8,128)(2,1)S(1)} %collective-permute-done.1), channel_id=1, source_target_pairs={{0,1},{1,2},{2,3},{3,4},{4,5},{5,6},{6,7},{7,0},{8,9},{9,10},{10,1... | collective-permute-start | bytes 3145736 | tf_op jit(solution)/shard_map/ppermute | solution.py:96
  55.8 1.0 copy-start.3
  56.8 16.0 %collective-permute-start.3 = (bf16[128,4096]{1,0:T(8,128)(2,1)S(1)}, bf16[128,4096]{1,0:T(8,128)(2,1)S(1)}, u32[]{:S(2)}, u32[]{:S(2)}) collective-permute-start(bf16[128,4096]{1,0:T(8,128)(2,1)S(1)} %collective-permute-done.2), channel_id=1, source_target_pairs={{0,1},{1,2},{2,3},{3,4},{4,5},{5,6},{6,7},{7,0},{8,9},{9,10},{10,1... | collective-permute-start | bytes 3145736 | tf_op jit(solution)/shard_map/ppermute | solution.py:96
  72.8 1.0 copy-start.5
  73.8 16.0 %collective-permute-start.4 = (bf16[128,4096]{1,0:T(8,128)(2,1)S(1)}, bf16[128,4096]{1,0:T(8,128)(2,1)S(1)}, u32[]{:S(2)}, u32[]{:S(2)}) collective-permute-start(bf16[128,4096]{1,0:T(8,128)(2,1)S(1)} %collective-permute-done.3), channel_id=1, source_target_pairs={{0,1},{1,2},{2,3},{3,4},{4,5},{5,6},{6,7},{7,0},{8,9},{9,10},{10,1... | collective-permute-start | bytes 3145736 | tf_op jit(solution)/shard_map/ppermute | solution.py:96
  89.9 28.6 %copy-start.7 = (bf16[128,4096]{1,0:T(8,128)(2,1)}, bf16[128,4096]{1,0:T(8,128)(2,1)S(1)}, u32[]{:S(2)}) copy-start(bf16[128,4096]{1,0:T(8,128)(2,1)S(1)} %collective-permute-done.4) | copy-start | bytes 3145732
  89.9 16.1 %collective-permute-start.5 = (bf16[128,4096]{1,0:T(8,128)(2,1)S(1)}, bf16[128,4096]{1,0:T(8,128)(2,1)}, u32[]{:S(2)}, u32[]{:S(2)}) collective-permute-start(bf16[128,4096]{1,0:T(8,128)(2,1)S(1)} %collective-permute-done.4), channel_id=1, source_target_pairs={{0,1},{1,2},{2,3},{3,4},{4,5},{5,6},{6,7},{7,0},{8,9},{9,10},{10,1... | collective-permute-start | bytes 3145736 | tf_op jit(solution)/shard_map/ppermute | solution.py:96
  91.8 14.3 %all-to-all-start = ((bf16[1,128,4,256]{1,3,0,2:T(8,128)(2,1)}), bf16[1,128,4,256]{1,3,0,2:T(8,128)(2,1)S(1)}, u32[]{:S(2)}, u32[]{:S(2)}) async-start(bf16[1,128,4,256]{1,3,0,2:T(8,128)(2,1)} %bitcast.128), calls=%async_computation | async-start | bytes 524288 | tf_op jit(solution)/shard_map/all_to_all | solution.py:44
  106.0 22.4 %collective-permute-start.6 = (bf16[128,4096]{1,0:T(8,128)(2,1)}, bf16[128,4096]{1,0:T(8,128)(2,1)}, u32[]{:S(2)}, u32[]{:S(2)}) collective-permute-start(bf16[128,4096]{1,0:T(8,128)(2,1)} %collective-permute-done.5), channel_id=1, source_target_pairs={{0,1},{1,2},{2,3},{3,4},{4,5},{5,6},{6,7},{7,0},{8,9},{9,10},{10,1... | collective-permute-start | bytes 3145736 | tf_op jit(solution)/shard_map/ppermute | solution.py:96
  106.2 12.3 %copy-start.9 = (bf16[1,128,4,256]{1,3,0,2:T(8,128)(2,1)}, bf16[1,128,4,256]{1,3,0,2:T(8,128)(2,1)S(1)}, u32[]{:S(2)}) copy-start(bf16[1,128,4,256]{1,3,0,2:T(8,128)(2,1)S(1)} %all-to-all-done) | copy-start | bytes 786436
  106.2 12.3 %all-to-all-start.1 = ((bf16[1,128,4,256]{1,3,0,2:T(8,128)(2,1)}), bf16[1,128,4,256]{1,3,0,2:T(8,128)(2,1)}, u32[]{:S(2)}, u32[]{:S(2)}) async-start(bf16[1,128,4,256]{1,3,0,2:T(8,128)(2,1)} %bitcast.129), calls=%async_computation.1 | async-start | bytes 524288 | tf_op jit(solution)/shard_map/all_to_all | solution.py:45
  118.4 72.2 %all-to-all-start.2 = ((bf16[1,128,4,1024]{1,3,0,2:T(8,128)(2,1)}), bf16[1,128,4,1024]{1,3,0,2:T(8,128)(2,1)S(1)}, u32[]{:S(2)}, u32[]{:S(2)}) async-start(bf16[1,128,4,1024]{1,3,0,2:T(8,128)(2,1)} %bitcast.123), calls=%async_computation.2 | async-start | bytes 2097152 | tf_op jit(solution)/shard_map/all_to_all | solution.py:43
  122.0 49.7 %all-gather.6.cloned.1.call-start = ((), (), s32[]{:S(2)}) async-start(), calls=%async_computation.7 | async-start | bytes 4718592 | tf_op jit(solution)/shard_map/all_gather | solution.py:55
  126.0 139.8 %reduce-scatter.5.cloned.1.call-start = ((), (), s32[]{:S(2)}) async-start(), calls=%async_computation.5 | async-start | bytes 5242880 | tf_op jit(solution)/shard_map/reduce_scatter | solution.py:108
  126.3 6.8 %copy-start.8 = (bf16[128,4096]{1,0:T(8,128)(2,1)S(1)}, bf16[128,4096]{1,0:T(8,128)(2,1)}, u32[]{:S(2)}) copy-start(bf16[128,4096]{1,0:T(8,128)(2,1)} %copy-done.7) | copy-start | bytes 3145732
  126.3 7.8 %copy-start.6 = (bf16[128,4096]{1,0:T(8,128)(2,1)S(1)}, bf16[128,4096]{1,0:T(8,128)(2,1)}, u32[]{:S(2)}) copy-start(bf16[128,4096]{1,0:T(8,128)(2,1)} %copy-done.5) | copy-start | bytes 3145732
  126.4 8.8 %copy-start.4 = (bf16[128,4096]{1,0:T(8,128)(2,1)S(1)}, bf16[128,4096]{1,0:T(8,128)(2,1)}, u32[]{:S(2)}) copy-start(bf16[128,4096]{1,0:T(8,128)(2,1)} %copy-done.3) | copy-start | bytes 3145732
  133.1 5.3 %copy-start.2 = (bf16[128,4096]{1,0:T(8,128)(2,1)S(1)}, bf16[128,4096]{1,0:T(8,128)(2,1)}, u32[]{:S(2)}) copy-start(bf16[128,4096]{1,0:T(8,128)(2,1)} %param.17) | copy-start | bytes 3145732
  193.2 6.5 %copy-start.10 = (bf16[5,4,128,256]{2,3,1,0:T(8,128)(2,1)S(1)}, bf16[5,4,128,256]{2,3,1,0:T(8,128)(2,1)}, u32[]{:S(2)}) copy-start(bf16[5,4,128,256]{2,3,1,0:T(8,128)(2,1)} %get-tuple-element.11) | copy-start | bytes 3932164
  204.7 10.1 %copy-start.12 = (s32[128,2]{0,1:T(2,128)S(1)}, s32[128,2]{0,1:T(2,128)}, u32[]{:S(2)}) copy-start(s32[128,2]{0,1:T(2,128)} %param.19) | copy-start | bytes 3076
  204.8 61.1 %copy-start = (bf16[128,4096]{1,0:T(8,128)(2,1)S(1)}, bf16[128,4096]{1,0:T(8,128)(2,1)}, u32[]{:S(2)}) copy-start(bf16[128,4096]{1,0:T(8,128)(2,1)} %param.12) | copy-start | bytes 3145732
  214.3 53.2 %copy-start.11 = (f32[4096]{0:T(1024)S(1)}, f32[4096]{0:T(1024)}, u32[]{:S(2)}) copy-start(f32[4096]{0:T(1024)} %param.18) | copy-start | bytes 49156
  214.3 112.1 %all-gather.4.cloned.1.call-start = ((), (), s32[]{:S(2)}) async-start(), calls=%async_computation.6 | async-start | bytes 5898240 | tf_op jit(solution)/shard_map/all_gather | solution.py:131
  270.2 178.3 %reduce-scatter.7.cloned.1.call-start = ((), (), s32[]{:S(2)}) async-start(), calls=%async_computation.8 | async-start | bytes 5898240
  389.8 0.7 copy-start.13
  389.8 61.1 %copy-start.1 = (bf16[128,4096]{1,0:T(8,128)(2,1)S(1)}, bf16[128,4096]{1,0:T(8,128)(2,1)}, u32[]{:S(2)}) copy-start(bf16[128,4096]{1,0:T(8,128)(2,1)} %reduce-scatter.5.cloned.1.call-done) | copy-start | bytes 3145732
Sparse Core Ops, SparseCore 0:
  126.1 45.4 all-gather.5
  214.4 51.3 reduce-scatter.4
  270.3 55.9 all-gather.3
  389.9 58.5 reduce-scatter.6
